TPU v7x, 32 devices: a whole 2x2x4 slice. The times are simulated.
32 devices in a mesh: wide: 8 (over z, y), blk: 4 (over x, core).
Axes of the slice: x: 2, y: 2, z: 4, core: 2. Of those that a mesh axis runs over, the one named last changes fastest.
Arguments:
- embeddings: bfloat16 [4096, 768], P(('wide', 'blk')), may hold values from -100 to 100
- bucket_ids: int32 [4096], P(('wide', 'blk')), may hold values from 0 to 7, as said below
- slot_ids: int32 [4096], P(('wide', 'blk')), may hold values from 0 to 31, as said below
- valid_rows: int32 [4096], P(('wide', 'blk')), may hold values 0 or 1
Outputs:
- neighbour_mean: bfloat16 [4096, 768], P(('wide', 'blk'))
- max_cosine: bfloat16 [4096], P(('wide', 'blk'))
Inputs may be any that keep to these rules, and one draw needn't show every extreme that they name: `bucket_ids`: bucket of each row. Every bucket holds at most 32 rows of one device; some bucket holds exactly 32 rows of every device. `slot_ids`: no two rows of one device share both bucket and slot.
All inputs are finite; a program needn't handle non-finite values. No bound on the sum of `valid_rows` on one device may be relied on, other than what follows from the above.
Results may differ from a plain program's by a relative error of at most 0.003.
Values may be sent and summed in bfloat16 or wider, within the bound.
A program may use at most 64 MiB of HBM per device.

v0:
```python
import jax
import jax.numpy as jnp
from jax import lax
from jax.sharding import PartitionSpec as P

sharpness = 10.0


def from_behind(value, axis, steps):
    count = lax.axis_size(axis)
    pairs = [(source, (source + steps) % count) for source in range(count)]
    return lax.ppermute(value, axis, pairs)


def unit_rows(embeddings):
    float_rows = embeddings.astype(jnp.float32)
    inverse_norm = lax.rsqrt(jnp.mean(float_rows * float_rows, axis=1, keepdims=True) + 1e-06)
    return (float_rows * inverse_norm).astype(jnp.bfloat16)


def bucket_stats(queries, query_pos, key_rows, key_flags, key_pos):
    feature_count = queries.shape[1]
    cosine = (
        lax.dot_general(
            queries, key_rows, (((1,), (1,)), ((), ())), preferred_element_type=jnp.float32
        )
        / feature_count
    )
    usable = (key_flags[None, :] > 0) & (query_pos[:, None] != key_pos[None, :])
    best_cos = jnp.max(jnp.where(usable, cosine, -1.0), axis=1)
    weights = jnp.where(usable, jnp.exp(sharpness * (cosine - 1.0)), 0.0)
    weight_total = jnp.sum(weights, axis=1)
    summed = jnp.dot(weights.astype(jnp.bfloat16), key_rows, preferred_element_type=jnp.float32)
    return (best_cos, weight_total, summed)


def on_device(embeddings, bucket_ids, slot_ids, valid_rows):
    unit_vectors = unit_rows(embeddings)
    row_count, feature_count = unit_vectors.shape
    groups = lax.axis_size("wide")
    blocks = lax.axis_size("blk")
    slot_count = 2 * row_count // groups
    block_rows = groups * slot_count
    cell_ids = bucket_ids * slot_count + slot_ids
    outgoing = jnp.zeros((block_rows, feature_count), jnp.bfloat16).at[cell_ids].set(unit_vectors)
    flag_rows = (
        jnp.zeros((block_rows,), jnp.bfloat16).at[cell_ids].set(valid_rows.astype(jnp.bfloat16))
    )
    arrived, arrived_flags = (
        lax.all_to_all(
            outgoing.reshape(groups, slot_count, feature_count),
            "wide",
            split_axis=0,
            concat_axis=0,
            tiled=True,
        ),
        lax.all_to_all(
            flag_rows.reshape(groups, slot_count), "wide", split_axis=0, concat_axis=0, tiled=True
        ),
    )
    queries = arrived.reshape(block_rows, feature_count)
    query_flags = arrived_flags.reshape(block_rows)
    my_block = lax.axis_index("blk")
    query_pos = my_block * block_rows + jnp.arange(block_rows, dtype=jnp.int32)

    def absorb(running, key_rows, key_flags, key_start):
        key_pos = key_start + jnp.arange(key_rows.shape[0], dtype=jnp.int32)
        best_cos, weight_total, summed = bucket_stats(
            queries, query_pos, key_rows, key_flags, key_pos
        )
        return (jnp.maximum(running[0], best_cos), running[1] + weight_total, running[2] + summed)

    initial = (
        jnp.full((block_rows,), -1.0, jnp.float32),
        jnp.zeros((block_rows,), jnp.float32),
        jnp.zeros((block_rows, feature_count), jnp.float32),
    )
    key_rows, key_flags = (queries, query_flags)
    running = absorb(initial, key_rows, key_flags, my_block * block_rows)
    for turn_index in range(1, blocks):
        key_rows, key_flags = from_behind((key_rows, key_flags), "blk", 1)
        running = absorb(
            running, key_rows, key_flags, (my_block - turn_index) % blocks * block_rows
        )
    best_cos, weight_total, summed = running
    mean_rows = ((queries.astype(jnp.float32) + summed) / (1.0 + weight_total[:, None])).astype(
        jnp.bfloat16
    )
    back_mean, back_best = (
        lax.all_to_all(
            mean_rows.reshape(groups, slot_count, feature_count),
            "wide",
            split_axis=0,
            concat_axis=0,
            tiled=True,
        ),
        lax.all_to_all(
            best_cos.astype(jnp.bfloat16).reshape(groups, slot_count),
            "wide",
            split_axis=0,
            concat_axis=0,
            tiled=True,
        ),
    )
    neighbour_mean = back_mean.reshape(block_rows, feature_count)[cell_ids]
    max_cosine = back_best.reshape(block_rows)[cell_ids]
    return (neighbour_mean, max_cosine)


def solution(mesh):
    in_specs = (
        P(("wide", "blk"), None),
        P(("wide", "blk")),
        P(("wide", "blk")),
        P(("wide", "blk")),
    )
    out_specs = (P(("wide", "blk"), None), P(("wide", "blk")))
    return jax.shard_map(
        on_device, mesh=mesh, in_specs=in_specs, out_specs=out_specs, check_vma=False
    )
```

profile of v0, /device:TPU:0, one launch (start us, length us, event | category | flops | bytes accessed | tf_op | source)
XLA Modules:
  0.0 79.2 jit_solution(11604375754238622393)
XLA Ops:
  0.7 0.7 convert_element_type.39
  1.4 1.3 %scatter_custom_fusion.1 = bf16[256]{0:T(256)(128)(2,1)S(1)} fusion(s32[128]{0:T(128)S(1)} %compare_select_fusion, bf16[128]{0:T(256)(128)(2,1)S(1)} %convert_element_type.39, bf16[]{:T(256)} %constant.53.clone.1), kind=kCustom, calls=%fused_computation.79 | custom fusion | bytes 514 | tf_op jit(solution)/shard_map/scatter | solution.py:47
  2.7 0.7 all_to_all.21
  3.4 7.3 %all-to-all-start.1 = ((bf16[8,1,32]{2,1,0:T(2,128)(2,1)}), bf16[8,1,32]{2,1,0:T(2,128)(2,1)S(1)}, u32[]{:S(2)}, u32[]{:S(2)}) async-start(bf16[8,1,32]{2,1,0:T(2,128)(2,1)} %all_to_all.21), calls=%async_computation.1 | async-start | bytes 8192 | tf_op jit(solution)/shard_map/all_to_all | solution.py:57
  10.7 1.0 %fusion.3 = f32[128]{0:T(128)S(1)} fusion(bf16[128,768]{1,0:T(8,128)(2,1)} %param.4), kind=kLoop, calls=%fused_computation.16 | loop fusion | flops 294784 | bytes 197120 | tf_op jit(solution)/shard_map/reduce_sum | solution.py:17
  11.8 1.9 %scatter_custom_fusion = bf16[256,768]{1,0:T(8,128)(2,1)} fusion(s32[128]{0:T(128)S(1)} %compare_select_fusion, bf16[128,768]{1,0:T(8,128)(2,1)S(1)} %copy-done, f32[128]{0:T(128)S(1)} %add_rsqrt_fusion, bf16[]{:T(256)} %constant.53.clone.1), kind=kCustom, calls=%fused_computation.30 | custom fusion | flops 294912 | bytes 590338 | tf_op jit(solution)/shard_map/scatter | solution.py:45
  13.7 3.4 %all-to-all-done.1 = bf16[8,1,32]{2,1,0:T(2,128)(2,1)S(1)} async-done(((bf16[8,1,32]{2,1,0:T(2,128)(2,1)}), bf16[8,1,32]{2,1,0:T(2,128)(2,1)S(1)}, u32[]{:S(2)}, u32[]{:S(2)}) %all-to-all-start.1) | async-done | bytes 544 | tf_op jit(solution)/shard_map/all_to_all | solution.py:57
  17.1 3.5 %all-to-all-start = ((bf16[8,32,768]{2,1,0:T(8,128)(2,1)}), bf16[8,32,768]{2,1,0:T(8,128)(2,1)S(1)}, u32[]{:S(2)}, u32[]{:S(2)}) async-start(bf16[8,32,768]{2,1,0:T(8,128)(2,1)} %bitcast), calls=%async_computation | async-start | bytes 786432 | tf_op jit(solution)/shard_map/all_to_all | solution.py:50
  20.8 10.2 %all-to-all-done = bf16[8,32,768]{2,1,0:T(8,128)(2,1)S(1)} async-done(((bf16[8,32,768]{2,1,0:T(8,128)(2,1)}), bf16[8,32,768]{2,1,0:T(8,128)(2,1)S(1)}, u32[]{:S(2)}, u32[]{:S(2)}) %all-to-all-start) | async-done | bytes 393248 | tf_op jit(solution)/shard_map/all_to_all | solution.py:50
  31.1 1.6 %collective-permute-start.2 = (bf16[256]{0:T(256)(128)(2,1)S(1)}, bf16[256]{0:T(256)(128)(2,1)S(1)}, u32[]{:S(2)}, u32[]{:S(2)}) collective-permute-start(bf16[256]{0:T(256)(128)(2,1)S(1)} %collective-permute-done), channel_id=1, source_target_pairs={{0,1},{1,2},{2,3},{3,0},{4,5},{5,6},{6,7},{7,4},{8,9},{9,10},{10,1... | collective-permute-start | bytes 1544 | tf_op jit(solution)/shard_map/ppermute | solution.py:12
  32.7 5.6 %collective-permute-done.2 = bf16[256]{0:T(256)(128)(2,1)S(1)} collective-permute-done((bf16[256]{0:T(256)(128)(2,1)S(1)}, bf16[256]{0:T(256)(128)(2,1)S(1)}, u32[]{:S(2)}, u32[]{:S(2)}) %collective-permute-start.2) | collective-permute-done | bytes 544 | tf_op jit(solution)/shard_map/ppermute | solution.py:12
  38.3 1.6 %collective-permute-start.3 = (bf16[256,768]{1,0:T(8,128)(2,1)S(1)}, bf16[256,768]{1,0:T(8,128)(2,1)S(1)}, u32[]{:S(2)}, u32[]{:S(2)}) collective-permute-start(bf16[256,768]{1,0:T(8,128)(2,1)S(1)} %collective-permute-done.1), channel_id=1, source_target_pairs={{0,1},{1,2},{2,3},{3,0},{4,5},{5,6},{6,7},{7,4},{8,9},{9,10},{10,1... | collective-permute-start | bytes 1179656 | tf_op jit(solution)/shard_map/ppermute | solution.py:12
  39.9 1.4 %collective-permute-done.4 = bf16[256]{0:T(256)(128)(2,1)S(1)} collective-permute-done((bf16[256]{0:T(256)(128)(2,1)S(1)}, bf16[256]{0:T(256)(128)(2,1)S(1)}, u32[]{:S(2)}, u32[]{:S(2)}) %collective-permute-start.4) | collective-permute-done | bytes 544 | tf_op jit(solution)/shard_map/ppermute | solution.py:12
  41.3 4.2 %collective-permute-done.3 = bf16[256,768]{1,0:T(8,128)(2,1)S(1)} collective-permute-done((bf16[256,768]{1,0:T(8,128)(2,1)S(1)}, bf16[256,768]{1,0:T(8,128)(2,1)S(1)}, u32[]{:S(2)}, u32[]{:S(2)}) %collective-permute-start.3) | collective-permute-done | bytes 393248 | tf_op jit(solution)/shard_map/ppermute | solution.py:12
  46.2 6.6 %collective-permute-done.5 = bf16[256,768]{1,0:T(8,128)(2,1)S(1)} collective-permute-done((bf16[256,768]{1,0:T(8,128)(2,1)S(1)}, bf16[256,768]{1,0:T(8,128)(2,1)S(1)}, u32[]{:S(2)}, u32[]{:S(2)}) %collective-permute-start.5) | collective-permute-done | bytes 393248 | tf_op jit(solution)/shard_map/ppermute | solution.py:12
  53.1 0.6 select_reduce_fusion.3
  53.7 0.7 max.42
  54.3 3.7 %all-to-all-start.3 = ((bf16[8,1,32]{2,1,0:T(2,128)(2,1)}), bf16[8,1,32]{2,1,0:T(2,128)(2,1)S(1)}, u32[]{:S(2)}, u32[]{:S(2)}) async-start(bf16[8,1,32]{2,1,0:T(2,128)(2,1)} %max.42), calls=%async_computation.3 | async-start | bytes 8192 | tf_op jit(solution)/shard_map/all_to_all | solution.py:97
  59.3 1.2 %fusion.2 = bf16[256,768]{1,0:T(8,128)(2,1)} fusion(f32[256,768]{1,0:T(8,128)S(1)} %convolution_add_fusion.1, bf16[256,768]{1,0:T(8,128)(2,1)S(1)} %collective-permute-done.5, bf16[256,768]{1,0:T(8,128)(2,1)S(1)} %bitcast.25, f32[256]{0:T(256)S(1)} %add_add_fusion, f32[256,256]{0,1:T(8,128)S(1)} %convolution_multiply_fusion, s32[256]{0:T(256)S(1)} %iota_add_fusion.3, ...), kind=kOutput, calls=%fused_computation.9 | convolution fusion | flops 102039552 | bytes 2231552 | tf_op jit(solution)/shard_map/dot_general | solution.py:33
  60.5 3.9 %all-to-all-done.3 = bf16[8,1,32]{2,1,0:T(2,128)(2,1)S(1)} async-done(((bf16[8,1,32]{2,1,0:T(2,128)(2,1)}), bf16[8,1,32]{2,1,0:T(2,128)(2,1)S(1)}, u32[]{:S(2)}, u32[]{:S(2)}) %all-to-all-start.3) | async-done | bytes 544 | tf_op jit(solution)/shard_map/all_to_all | solution.py:97
  64.4 3.5 %all-to-all-start.2 = ((bf16[8,32,768]{2,1,0:T(8,128)(2,1)}), bf16[8,32,768]{2,1,0:T(8,128)(2,1)S(1)}, u32[]{:S(2)}, u32[]{:S(2)}) async-start(bf16[8,32,768]{2,1,0:T(8,128)(2,1)} %bitcast.2), calls=%async_computation.2 | async-start | bytes 786432 | tf_op jit(solution)/shard_map/all_to_all | solution.py:90
  68.0 1.7 %gather_fusion.1 = bf16[128]{0:T(256)(128)(2,1)} fusion(bf16[256]{0:T(256)(128)(2,1)S(1)} %reshape.141, s32[1024]{0:T(1024)S(1)} %pad_clamp_fusion), kind=kCustom, calls=%fused_computation.1 | custom fusion | bytes 1024 | tf_op jit(solution)/shard_map/gather | solution.py:106
  69.7 7.9 %all-to-all-done.2 = bf16[8,32,768]{2,1,0:T(8,128)(2,1)S(1)} async-done(((bf16[8,32,768]{2,1,0:T(8,128)(2,1)}), bf16[8,32,768]{2,1,0:T(8,128)(2,1)S(1)}, u32[]{:S(2)}, u32[]{:S(2)}) %all-to-all-start.2) | async-done | bytes 393248 | tf_op jit(solution)/shard_map/all_to_all | solution.py:90
  77.6 1.5 %gather_fusion = bf16[128,768]{1,0:T(8,128)(2,1)} fusion(bf16[256,768]{1,0:T(8,128)(2,1)S(1)} %bitcast.18, s32[1024]{0:T(1024)S(1)} %pad_clamp_fusion), kind=kCustom, calls=%fused_computation | custom fusion | bytes 393728 | tf_op jit(solution)/shard_map/gather | solution.py:105
  (35 shorter events, 2.5 us)
Async XLA Ops:
  0.6 0.7 copy-start.1
  0.6 0.7 copy-start.2
  0.7 11.1 %copy-start = (bf16[128,768]{1,0:T(8,128)(2,1)S(1)}, bf16[128,768]{1,0:T(8,128)(2,1)}, u32[]{:S(2)}) copy-start(bf16[128,768]{1,0:T(8,128)(2,1)} %param.4) | copy-start | bytes 589828
  3.4 13.7 %all-to-all-start.1 = ((bf16[8,1,32]{2,1,0:T(2,128)(2,1)}), bf16[8,1,32]{2,1,0:T(2,128)(2,1)S(1)}, u32[]{:S(2)}, u32[]{:S(2)}) async-start(bf16[8,1,32]{2,1,0:T(2,128)(2,1)} %all_to_all.21), calls=%async_computation.1 | async-start | bytes 8192 | tf_op jit(solution)/shard_map/all_to_all | solution.py:57
  17.1 13.9 %all-to-all-start = ((bf16[8,32,768]{2,1,0:T(8,128)(2,1)}), bf16[8,32,768]{2,1,0:T(8,128)(2,1)S(1)}, u32[]{:S(2)}, u32[]{:S(2)}) async-start(bf16[8,32,768]{2,1,0:T(8,128)(2,1)} %bitcast), calls=%async_computation | async-start | bytes 786432 | tf_op jit(solution)/shard_map/all_to_all | solution.py:50
  20.8 10.2 %collective-permute-start = (bf16[256]{0:T(256)(128)(2,1)S(1)}, bf16[256]{0:T(256)(128)(2,1)S(1)}, u32[]{:S(2)}, u32[]{:S(2)}) collective-permute-start(bf16[256]{0:T(256)(128)(2,1)S(1)} %broadcast_in_dim_reshape.3), channel_id=1, source_target_pairs={{0,1},{1,2},{2,3},{3,0},{4,5},{5,6},{6,7},{7,4},{8,9},{9,10},{10,1... | collective-permute-start | bytes 1544 | tf_op jit(solution)/shard_map/ppermute | solution.py:12
  31.0 7.3 %collective-permute-start.1 = (bf16[256,768]{1,0:T(8,128)(2,1)S(1)}, bf16[256,768]{1,0:T(8,128)(2,1)S(1)}, u32[]{:S(2)}, u32[]{:S(2)}) collective-permute-start(bf16[256,768]{1,0:T(8,128)(2,1)S(1)} %bitcast.19), channel_id=1, source_target_pairs={{0,1},{1,2},{2,3},{3,0},{4,5},{5,6},{6,7},{7,4},{8,9},{9,10},{10,1... | collective-permute-start | bytes 1179656 | tf_op jit(solution)/shard_map/ppermute | solution.py:12
  31.1 7.3 %collective-permute-start.2 = (bf16[256]{0:T(256)(128)(2,1)S(1)}, bf16[256]{0:T(256)(128)(2,1)S(1)}, u32[]{:S(2)}, u32[]{:S(2)}) collective-permute-start(bf16[256]{0:T(256)(128)(2,1)S(1)} %collective-permute-done), channel_id=1, source_target_pairs={{0,1},{1,2},{2,3},{3,0},{4,5},{5,6},{6,7},{7,4},{8,9},{9,10},{10,1... | collective-permute-start | bytes 1544 | tf_op jit(solution)/shard_map/ppermute | solution.py:12
  38.3 3.0 %collective-permute-start.4 = (bf16[256]{0:T(256)(128)(2,1)S(1)}, bf16[256]{0:T(256)(128)(2,1)S(1)}, u32[]{:S(2)}, u32[]{:S(2)}) collective-permute-start(bf16[256]{0:T(256)(128)(2,1)S(1)} %collective-permute-done.2), channel_id=1, source_target_pairs={{0,1},{1,2},{2,3},{3,0},{4,5},{5,6},{6,7},{7,4},{8,9},{9,10},{10,1... | collective-permute-start | bytes 1544 | tf_op jit(solution)/shard_map/ppermute | solution.py:12
  38.3 7.2 %collective-permute-start.3 = (bf16[256,768]{1,0:T(8,128)(2,1)S(1)}, bf16[256,768]{1,0:T(8,128)(2,1)S(1)}, u32[]{:S(2)}, u32[]{:S(2)}) collective-permute-start(bf16[256,768]{1,0:T(8,128)(2,1)S(1)} %collective-permute-done.1), channel_id=1, source_target_pairs={{0,1},{1,2},{2,3},{3,0},{4,5},{5,6},{6,7},{7,4},{8,9},{9,10},{10,1... | collective-permute-start | bytes 1179656 | tf_op jit(solution)/shard_map/ppermute | solution.py:12
  45.6 7.2 %collective-permute-start.5 = (bf16[256,768]{1,0:T(8,128)(2,1)S(1)}, bf16[256,768]{1,0:T(8,128)(2,1)S(1)}, u32[]{:S(2)}, u32[]{:S(2)}) collective-permute-start(bf16[256,768]{1,0:T(8,128)(2,1)S(1)} %collective-permute-done.3), channel_id=1, source_target_pairs={{0,1},{1,2},{2,3},{3,0},{4,5},{5,6},{6,7},{7,4},{8,9},{9,10},{10,1... | collective-permute-start | bytes 1179656 | tf_op jit(solution)/shard_map/ppermute | solution.py:12
  54.3 10.1 %all-to-all-start.3 = ((bf16[8,1,32]{2,1,0:T(2,128)(2,1)}), bf16[8,1,32]{2,1,0:T(2,128)(2,1)S(1)}, u32[]{:S(2)}, u32[]{:S(2)}) async-start(bf16[8,1,32]{2,1,0:T(2,128)(2,1)} %max.42), calls=%async_computation.3 | async-start | bytes 8192 | tf_op jit(solution)/shard_map/all_to_all | solution.py:97
  64.4 13.2 %all-to-all-start.2 = ((bf16[8,32,768]{2,1,0:T(8,128)(2,1)}), bf16[8,32,768]{2,1,0:T(8,128)(2,1)S(1)}, u32[]{:S(2)}, u32[]{:S(2)}) async-start(bf16[8,32,768]{2,1,0:T(8,128)(2,1)} %bitcast.2), calls=%async_computation.2 | async-start | bytes 786432 | tf_op jit(solution)/shard_map/all_to_all | solution.py:90
where the time goes:
time: 79.6 us; the launch traced here: 79.2 us
  waiting for transfers between devices  43.3 us (54%)
  starting transfers between devices  21.1 us (27%)
  local copies, waits for them, and re-layouts  6.16 us (8%)
  matrix products  3.92 us (5%)
  other arithmetic  3.81 us (5%)
  between operations  0.86 us (1%)
    ppermute x6, waiting for transfers between devices, from_behind(): return lax.ppermute(value, axis, pairs)  17.8 us
    all_to_all x1, waiting for transfers between devices, on_device(): lax.all_to_all(outgoing.reshape(groups, slot_count, feature_count), 'wide...  10.2 us
    all_to_all x1, waiting for transfers between devices, on_device(): lax.all_to_all(mean_rows.reshape(groups, slot_count, feature_count), 'wid...  7.88 us
    all_to_all x1, starting transfers between devices, on_device(): lax.all_to_all(flag_rows.reshape(groups, slot_count), 'wide', split_axis=...  7.31 us
    all_to_all x1, waiting for transfers between devices, on_device(): lax.all_to_all(best_cos.astype(jnp.bfloat16).reshape(groups, slot_count),...  3.94 us
    all_to_all x1, starting transfers between devices, on_device(): lax.all_to_all(best_cos.astype(jnp.bfloat16).reshape(groups, slot_count),...  3.66 us
    all_to_all x1, starting transfers between devices, on_device(): lax.all_to_all(outgoing.reshape(groups, slot_count, feature_count), 'wide...  3.45 us
    all_to_all x1, starting transfers between devices, on_device(): lax.all_to_all(mean_rows.reshape(groups, slot_count, feature_count), 'wid...  3.45 us
  transfers between devices with their start and end apart: 10, of which 8 were waited for; matrix products, arithmetic and copies ran while one was open for 10% of the time, Pallas kernels for 0%

commit v1 on v0

--- a/solution.py
+++ b/solution.py
@@ -1,6 +1,10 @@
+import functools
+
 import jax
 import jax.numpy as jnp
 from jax import lax
+from jax.experimental import pallas as pl
+from jax.experimental.pallas import tpu as pltpu
 from jax.sharding import PartitionSpec as P
 
 sharpness = 10.0
@@ -34,7 +38,7 @@
     return (best_cos, weight_total, summed)
 
 
-def on_device(embeddings, bucket_ids, slot_ids, valid_rows):
+def by_bucket(embeddings, bucket_ids, slot_ids, valid_rows):
     unit_vectors = unit_rows(embeddings)
     row_count, feature_count = unit_vectors.shape
     groups = lax.axis_size("wide")
@@ -107,6 +111,344 @@
     return (neighbour_mean, max_cosine)
 
 
+PAIR = 2
+PIECES = 2
+
+
+def arrival_order(place, count):
+    low, high = place, count - 1 - place
+    order = []
+    for distance in range(1, count):
+        if distance <= low:
+            order.append(place - distance)
+        if distance <= high:
+            order.append(place + distance)
+    return order
+
+
+def dense_kernel(
+    planes, emb_ref, bucket_ref, valid_ref, mean_ref, best_ref,
+    keys, key_meta, queries, query_meta, query_col, total, peak, weight,
+    part_out, part_in, stat_out, stat_in,
+    z_send, z_recv, zm_send, zm_recv, c_send, c_recv, cm_send, cm_recv,
+    q_send, q_recv, qm_send, qm_recv, p_send, p_recv, s_send, s_recv,
+):
+    rows, features = emb_ref.shape
+    spots = queries.shape[0]
+    wide, blk = lax.axis_index("wide"), lax.axis_index("blk")
+    z, y = lax.div(wide, PAIR), lax.rem(wide, PAIR)
+    x, core = lax.div(blk, PAIR), lax.rem(blk, PAIR)
+    other = 1 - core
+    columns = spots // PAIR
+    piece = rows // PIECES
+
+    def at(z_at, y_at, x_at, core_at):
+        return (z_at * PAIR + y_at, x_at * PAIR + core_at)
+
+    def spot_device(spot):
+        dy, dx = divmod(spot, columns)
+        return at(z, lax.rem(y + dy, PAIR), lax.rem(x + dx, columns), core)
+
+    def seen_from(spot):
+        dy, dx = divmod(spot, columns)
+        return (-dy) % PAIR * columns + (-dx) % columns
+
+    def remote(source, target, send, recv, device):
+        return pltpu.make_async_remote_copy(
+            src_ref=source, dst_ref=target, send_sem=send, recv_sem=recv,
+            device_id=device, device_id_type=pl.DeviceIdType.MESH,
+        )
+
+    partner = at(z, y, x, other)
+    has_low, has_high = z > 0, z < planes - 1
+
+    barrier = pltpu.get_barrier_semaphore()
+
+    def greet(device):
+        pl.semaphore_signal(barrier, inc=1, device_id=device, device_id_type=pl.DeviceIdType.MESH)
+
+    greet(partner)
+    for spot in range(1, spots):
+        greet(spot_device(spot))
+
+    @pl.when(has_low)
+    def _():
+        greet(at(z - 1, y, x, core))
+
+    @pl.when(has_high)
+    def _():
+        greet(at(z + 1, y, x, core))
+
+    floats = emb_ref[...].astype(jnp.float32)
+    inverse = lax.rsqrt(jnp.mean(floats * floats, axis=1, keepdims=True) + 1e-06)
+    unit = (floats * inverse).astype(jnp.bfloat16)
+    keys[z, core] = unit
+    queries[0] = unit
+    meta = jnp.concatenate([bucket_ref[...], valid_ref[...]], axis=0).astype(jnp.float32)
+    key_meta[z, core] = meta
+    query_meta[0] = meta
+
+    pl.semaphore_wait(barrier, jnp.where(has_low & has_high, spots + 2, spots + 1))
+
+    def z_meta(source, way, to):
+        ref = key_meta.at[source, core]
+        return remote(
+            ref, ref, zm_send.at[source, way], zm_recv.at[source], at(to, y, x, core)
+        )
+
+    def z_copy(source, way, to, part):
+        ref = keys.at[source, core, pl.ds(part * piece, piece)]
+        return remote(
+            ref, ref, z_send.at[source, way, part], z_recv.at[source, part], at(to, y, x, core)
+        )
+
+    def c_meta(source, side):
+        ref = key_meta.at[source, side]
+        return remote(ref, ref, cm_send.at[source], cm_recv.at[source], partner)
+
+    def c_copy(source, side, part):
+        ref = keys.at[source, side, pl.ds(part * piece, piece)]
+        return remote(ref, ref, c_send.at[source, part], c_recv.at[source, part], partner)
+
+    def q_meta(spot):
+        mine = seen_from(spot)
+        return remote(
+            query_meta.at[0], query_meta.at[mine], qm_send.at[spot], qm_recv.at[mine],
+            spot_device(spot),
+        )
+
+    def q_copy(spot):
+        mine = seen_from(spot)
+        return remote(
+            queries.at[0], queries.at[mine], q_send.at[spot], q_recv.at[mine], spot_device(spot)
+        )
+
+    def send_ways(source, act):
+        @pl.when((source <= z) & has_high)
+        def _():
+            act(1, z + 1)
+
+        @pl.when((source >= z) & has_low)
+        def _():
+            act(0, z - 1)
+
+    send_ways(z, lambda way, to: z_meta(z, way, to).start())
+    for part in range(PIECES):
+        send_ways(z, lambda way, to: z_copy(z, way, to, part).start())
+    c_meta(z, core).start()
+    for part in range(PIECES):
+        c_copy(z, core, part).start()
+    for spot in range(spots - 1, 0, -1):
+        q_meta(spot).start()
+        q_copy(spot).start()
+
+    def column_of(spot):
+        row = query_meta[spot, 0:1, :]
+        query_col[spot] = jnp.transpose(jnp.broadcast_to(row, (rows, rows)))
+
+    def absorb(first, last, source, fresh):
+        count = (last - first) * rows
+        chosen = queries[first:last].reshape(count, features)
+        block = keys[source].reshape(PAIR * rows, features)
+        cosine = lax.dot_general(
+            chosen, block, (((1,), (1,)), ((), ())), preferred_element_type=jnp.float32
+        ) * (1.0 / features)
+        buckets = query_col[first:last].reshape(count, rows)
+        line = lax.broadcasted_iota(jnp.int32, (count, rows), 0)
+        lane = lax.broadcasted_iota(jnp.int32, (count, rows), 1)
+        factors = []
+        peaks = None
+        sums = None
+        for side in range(PAIR):
+            key_bucket = key_meta[source, side, 0:1, :]
+            key_flag = key_meta[source, side, 1:2, :]
+            wanted = jnp.where(key_flag > 0, key_bucket, -1.0)
+            usable = buckets == wanted
+            if first == 0:
+                own = (source == z) & (core == side)
+                shift = jnp.where(own, 0, count + rows)
+                usable = usable & (line + shift != lane)
+            values = cosine[:, side * rows : (side + 1) * rows]
+            best = jnp.where(usable, values, -1.0)
+            factor = jnp.where(usable, jnp.exp(sharpness * (values - 1.0)), 0.0)
+            factors.append(factor.astype(jnp.bfloat16))
+            peaks = best if peaks is None else jnp.maximum(peaks, best)
+            sums = factor if sums is None else sums + factor
+        summed = jnp.dot(
+            jnp.concatenate(factors, axis=1), block, preferred_element_type=jnp.float32
+        )
+        part = (last - first, rows)
+        if fresh:
+            peak[first:last] = peaks.reshape(*part, rows)
+            weight[first:last] = sums.reshape(*part, rows)
+            total[first:last] = summed.reshape(*part, features)
+        else:
+            peak[first:last] = jnp.maximum(peak[first:last], peaks.reshape(*part, rows))
+            weight[first:last] += sums.reshape(*part, rows)
+            total[first:last] += summed.reshape(*part, features)
+
+    def wait_partner(source):
+        c_meta(source, other).wait_recv()
+        for part in range(PIECES):
+            c_copy(source, other, part).wait_recv()
+
+    def take(source):
+        z_meta(source, 0, z).wait_recv()
+        send_ways(source, lambda way, to: z_meta(source, way, to).start())
+        c_meta(source, core).start()
+        for part in range(PIECES):
+            z_copy(source, 0, z, part).wait_recv()
+            send_ways(source, lambda way, to: z_copy(source, way, to, part).start())
+            c_copy(source, core, part).start()
+
+    orders = [arrival_order(place, planes) for place in range(planes)]
+
+    def source_at(turn):
+        source = jnp.int32(orders[0][turn])
+        for place in range(1, planes):
+            source = jnp.where(z == place, orders[place][turn], source)
+        return source
+
+    sources = [source_at(turn) for turn in range(planes - 1)]
+    inner = has_low & has_high
+
+    column_of(0)
+    wait_partner(z)
+    absorb(0, 1, z, True)
+    for source in sources[:-1]:
+        take(source)
+        wait_partner(source)
+        absorb(0, 1, source, False)
+    final = sources[-1]
+
+    @pl.when(inner)
+    def _():
+        take(final)
+
+    for spot in range(1, spots):
+        q_meta(seen_from(spot)).wait_recv()
+        column_of(spot)
+        q_copy(seen_from(spot)).wait_recv()
+    absorb(1, spots, z, True)
+    for source in sources[:-1]:
+        absorb(1, spots, source, False)
+
+    @pl.when(jnp.logical_not(inner))
+    def _():
+        take(final)
+
+    wait_partner(final)
+    absorb(0, spots, final, False)
+
+    def stat_rows(spot):
+        top = jnp.max(jnp.transpose(peak[spot]), axis=0, keepdims=True)
+        mass = jnp.sum(jnp.transpose(weight[spot]), axis=0, keepdims=True)
+        return top, mass
+
+    def p_copy(spot):
+        mine = seen_from(spot)
+        return remote(
+            part_out.at[spot], part_in.at[mine], p_send.at[spot], p_recv.at[mine],
+            spot_device(spot),
+        )
+
+    def s_copy(spot):
+        mine = seen_from(spot)
+        return remote(
+            stat_out.at[spot], stat_in.at[mine], s_send.at[spot], s_recv.at[mine],
+            spot_device(spot),
+        )
+
+    for spot in range(spots - 1, 0, -1):
+        part_out[spot] = total[spot].astype(jnp.bfloat16)
+        p_copy(spot).start()
+    for spot in range(spots - 1, 0, -1):
+        stat_out[spot] = jnp.concatenate(stat_rows(spot), axis=0)
+        s_copy(spot).start()
+
+    top, mass = stat_rows(0)
+    result = total[0] + queries[0].astype(jnp.float32)
+    for spot in range(1, spots):
+        s_copy(seen_from(spot)).wait_recv()
+        top = jnp.maximum(top, stat_in[spot, 0:1, :])
+        mass = mass + stat_in[spot, 1:2, :]
+    best_ref[...] = top.astype(jnp.bfloat16)
+    below = jnp.transpose(jnp.broadcast_to(1.0 + mass, (rows, rows)))[:, 0:1]
+    for spot in range(1, spots):
+        p_copy(seen_from(spot)).wait_recv()
+        result = result + part_in[spot].astype(jnp.float32)
+    mean_ref[...] = (result / below).astype(jnp.bfloat16)
+
+    send_ways(z, lambda way, to: z_meta(z, way, to).wait_send())
+    for part in range(PIECES):
+        send_ways(z, lambda way, to: z_copy(z, way, to, part).wait_send())
+    c_meta(z, core).wait_send()
+    for part in range(PIECES):
+        c_copy(z, core, part).wait_send()
+    for source in sources:
+        send_ways(source, lambda way, to: z_meta(source, way, to).wait_send())
+        c_meta(source, core).wait_send()
+        for part in range(PIECES):
+            send_ways(source, lambda way, to: z_copy(source, way, to, part).wait_send())
+            c_copy(source, core, part).wait_send()
+    for spot in range(1, spots):
+        q_meta(spot).wait_send()
+        q_copy(spot).wait_send()
+        p_copy(spot).wait_send()
+        s_copy(spot).wait_send()
+
+
+def dense(embeddings, bucket_ids, valid_rows):
+    rows, features = embeddings.shape
+    planes = lax.axis_size("wide") // PAIR
+    spots = lax.axis_size("blk")
+    dma = pltpu.SemaphoreType.DMA
+    vmem = pl.BlockSpec(memory_space=pltpu.VMEM)
+    mean, best = pl.pallas_call(
+        functools.partial(dense_kernel, planes),
+        out_shape=(
+            jax.ShapeDtypeStruct((rows, features), jnp.bfloat16),
+            jax.ShapeDtypeStruct((1, rows), jnp.bfloat16),
+        ),
+        in_specs=[vmem] * 3,
+        out_specs=(vmem, vmem),
+        scratch_shapes=[
+            pltpu.VMEM((planes, PAIR, rows, features), jnp.bfloat16),
+            pltpu.VMEM((planes, PAIR, 2, rows), jnp.float32),
+            pltpu.VMEM((spots, rows, features), jnp.bfloat16),
+            pltpu.VMEM((spots, 2, rows), jnp.float32),
+            pltpu.VMEM((spots, rows, rows), jnp.float32),
+            pltpu.VMEM((spots, rows, features), jnp.float32),
+            pltpu.VMEM((spots, rows, rows), jnp.float32),
+            pltpu.VMEM((spots, rows, rows), jnp.float32),
+            pltpu.VMEM((spots, rows, features), jnp.bfloat16),
+            pltpu.VMEM((spots, rows, features), jnp.bfloat16),
+            pltpu.VMEM((spots, 2, rows), jnp.float32),
+            pltpu.VMEM((spots, 2, rows), jnp.float32),
+            dma((planes, 2, PIECES)), dma((planes, PIECES)), dma((planes, 2)), dma((planes,)),
+            dma((planes, PIECES)), dma((planes, PIECES)), dma((planes,)), dma((planes,)),
+            dma((spots,)), dma((spots,)), dma((spots,)), dma((spots,)),
+            dma((spots,)), dma((spots,)), dma((spots,)), dma((spots,)),
+        ],
+        compiler_params=pltpu.CompilerParams(
+            collective_id=0, has_side_effects=True, vmem_limit_bytes=56 * 1024 * 1024
+        ),
+    )(embeddings, bucket_ids.reshape(1, rows), valid_rows.reshape(1, rows))
+    return mean, best.reshape(rows)
+
+
+def on_device(embeddings, bucket_ids, slot_ids, valid_rows):
+    rows = embeddings.shape[0]
+    groups = lax.axis_size("wide")
+    blocks = lax.axis_size("blk")
+    bucket_work = blocks * (2 * rows) ** 2
+    dense_work = groups * blocks * rows**2
+    fits = groups % PAIR == 0 and groups > PAIR and blocks == PAIR * PAIR and rows == 128
+    if fits and dense_work <= 4 * bucket_work:
+        return dense(embeddings, bucket_ids, valid_rows)
+    return by_bucket(embeddings, bucket_ids, slot_ids, valid_rows)
+
+
 def solution(mesh):
     in_specs = (
         P(("wide", "blk"), None),

time: 79.6 us -> 41.6 us (0.52)
  waiting for transfers between devices: 43.3 us -> 0 us
  Pallas kernels: 0 us -> 38.7 us
  starting transfers between devices: 21.1 us -> 0 us
  local copies, waits for them, and re-layouts: 6.16 us -> 2.13 us
  matrix products: 3.92 us -> 0 us
  other arithmetic: 3.81 us -> 0 us
    pallas_call x0 -> x1, Pallas kernels: none -> 38.7 us  [dense(): pl.pallas_call(functools.partial(dense_kernel, planes), out_shape=(jax.Sh...]
    all_to_all x4 -> x0, waiting for transfers between devices: 25.5 us -> none  [the longest x1 10.2 us: on_device(): lax.all_to_all(outgoing.reshape(groups, slot_count, feature_count), 'wide...]
    all_to_all x4 -> x0, starting transfers between devices: 17.9 us -> none  [the longest x1 7.31 us: on_device(): lax.all_to_all(flag_rows.reshape(groups, slot_count), 'wide', split_axis=...]
    ppermute x6 -> x0, waiting for transfers between devices: 17.8 us -> none  [from_behind(): return lax.ppermute(value, axis, pairs)]
    dot_general x8 -> x0, matrix products: 3.92 us -> none  [the longest x4 2.44 us: bucket_stats(): jnp.dot(weights.astype(jnp.bfloat16), key_rows, preferred_element_type=jn...]
    gather x2 -> x0, local copies, waits for them, and re-layouts: 3.27 us -> none  [the longest x1 1.73 us: on_device(): max_cosine = back_best.reshape(block_rows)[cell_ids]]
    ppermute x6 -> x0, starting transfers between devices: 3.26 us -> none  [from_behind(): return lax.ppermute(value, axis, pairs)]
    unnamed x6 -> x4, local copies, waits for them, and re-layouts: 0.01 us -> 2.13 us
  transfers between devices with their start and end apart: 10 -> 0, of which waited for: 8 -> 0; matrix products, arithmetic and copies ran while one was open for 10% -> 0% of each run, Pallas kernels for 0% -> 0%
where the time goes in v1:
time: 41.6 us; the launch traced here: 41.4 us
  Pallas kernels  38.7 us (93%)
  local copies, waits for them, and re-layouts  2.13 us (5%)
  between operations  0.65 us (2%)
    pallas_call x1, Pallas kernels, dense(): pl.pallas_call(functools.partial(dense_kernel, planes), out_shape=(jax.Sh...  38.7 us
    unnamed x4, local copies, waits for them, and re-layouts  2.13 us

profile of v1, /device:TPU:0, one launch (start us, length us, event | category | flops | bytes accessed | tf_op | source)
XLA Modules:
  0.0 41.4 jit_solution(18311174952001784555)
XLA Ops:
  0.6 38.7 %shard_map.50 = (bf16[128,768]{1,0:T(8,128)(2,1)}, bf16[1,128]{1,0:T(2,128)(2,1)}) custom-call(bf16[128,768]{1,0:T(8,128)(2,1)} %emb_ref.1, s32[1,128]{1,0:T(1,128)} %bitcast.3, s32[1,128]{1,0:T(1,128)} %bitcast.4), custom_call_target="tpu_custom_call" | custom-call | tf_op jit(solution)/shard_map/pallas_call | solution.py:407
  39.3 0.0 copy-start
  39.3 1.6 %copy.7 = bf16[128,768]{1,0:T(8,128)(2,1)} copy(bf16[128,768]{1,0:T(8,128)(2,1)} %get-tuple-element.8) | data formatting | bytes 393216
  40.9 0.0 copy-done
  40.9 0.5 %copy.8 = bf16[128]{0:T(256)(128)(2,1)} copy(bf16[128]{0:T(256)(128)(2,1)S(1)} %bitcast.5) | data formatting | bytes 512
Async XLA Ops:
  39.3 1.6 %copy-start = (bf16[1,128]{1,0:T(2,128)(2,1)S(1)}, bf16[1,128]{1,0:T(2,128)(2,1)}, u32[]{:S(2)}) copy-start(bf16[1,128]{1,0:T(2,128)(2,1)} %get-tuple-element.5) | copy-start | bytes 772

commit v2 on v1

--- a/solution.py
+++ b/solution.py
@@ -112,7 +112,7 @@
 
 
 PAIR = 2
-PIECES = 2
+PIECES = 4
 
 
 def arrival_order(place, count):
@@ -292,14 +292,16 @@
         for part in range(PIECES):
             c_copy(source, other, part).wait_recv()
 
-    def take(source):
-        z_meta(source, 0, z).wait_recv()
-        send_ways(source, lambda way, to: z_meta(source, way, to).start())
-        c_meta(source, core).start()
+    def take(*arriving):
+        for source in arriving:
+            z_meta(source, 0, z).wait_recv()
+            send_ways(source, lambda way, to: z_meta(source, way, to).start())
+            c_meta(source, core).start()
         for part in range(PIECES):
-            z_copy(source, 0, z, part).wait_recv()
-            send_ways(source, lambda way, to: z_copy(source, way, to, part).start())
-            c_copy(source, core, part).start()
+            for source in arriving:
+                z_copy(source, 0, z, part).wait_recv()
+                send_ways(source, lambda way, to: z_copy(source, way, to, part).start())
+                c_copy(source, core, part).start()
 
     orders = [arrival_order(place, planes) for place in range(planes)]
 
@@ -311,19 +313,27 @@
 
     sources = [source_at(turn) for turn in range(planes - 1)]
     inner = has_low & has_high
+    final = sources[-1]
+
+    def at_end(source):
+        @pl.when(jnp.logical_not(inner))
+        def _():
+            take(source)
 
     column_of(0)
     wait_partner(z)
     absorb(0, 1, z, True)
+
+    @pl.when(inner)
+    def _():
+        take(*sources[:2])
+        for source in sources[2:]:
+            take(source)
+
     for source in sources[:-1]:
-        take(source)
+        at_end(source)
         wait_partner(source)
         absorb(0, 1, source, False)
-    final = sources[-1]
-
-    @pl.when(inner)
-    def _():
-        take(final)
 
     for spot in range(1, spots):
         q_meta(seen_from(spot)).wait_recv()
@@ -332,24 +342,31 @@
     absorb(1, spots, z, True)
     for source in sources[:-1]:
         absorb(1, spots, source, False)
-
-    @pl.when(jnp.logical_not(inner))
-    def _():
-        take(final)
-
+    at_end(final)
     wait_partner(final)
-    absorb(0, spots, final, False)
 
     def stat_rows(spot):
         top = jnp.max(jnp.transpose(peak[spot]), axis=0, keepdims=True)
         mass = jnp.sum(jnp.transpose(weight[spot]), axis=0, keepdims=True)
         return top, mass
 
-    def p_copy(spot):
+    across, along = columns, 1
+    corner = across + along
+    half = rows // 2
+    halves = (pl.ds(0, half), pl.ds(half, half))
+
+    def p_copy(spot, side):
         mine = seen_from(spot)
         return remote(
-            part_out.at[spot], part_in.at[mine], p_send.at[spot], p_recv.at[mine],
-            spot_device(spot),
+            part_out.at[spot, halves[side]], part_in.at[mine, halves[side]],
+            p_send.at[spot, side], p_recv.at[mine, side], spot_device(spot),
+        )
+
+    def corner_copy(side):
+        spot = (along, across)[side]
+        return remote(
+            part_out.at[corner, halves[side]], part_in.at[corner, halves[side]],
+            p_send.at[corner, side], p_recv.at[corner, side], spot_device(spot),
         )
 
     def s_copy(spot):
@@ -359,23 +376,39 @@
             spot_device(spot),
         )
 
-    for spot in range(spots - 1, 0, -1):
-        part_out[spot] = total[spot].astype(jnp.bfloat16)
-        p_copy(spot).start()
+    absorb(corner, corner + 1, final, False)
+    part_out[corner] = total[corner].astype(jnp.bfloat16)
+    corner_copy(0).start()
+    corner_copy(1).start()
+    passing = ((along, 1), (across, 0))
+    for spot, side in passing:
+        absorb(spot, spot + 1, final, False)
+        part_out[spot, halves[1 - side]] = total[spot, halves[1 - side]].astype(jnp.bfloat16)
+        p_copy(spot, 1 - side).start()
     for spot in range(spots - 1, 0, -1):
         stat_out[spot] = jnp.concatenate(stat_rows(spot), axis=0)
         s_copy(spot).start()
-
+    for spot, side in passing:
+        corner_copy(side).wait_recv()
+        part_out[spot, halves[side]] = (
+            total[spot, halves[side]] + part_in[corner, halves[side]].astype(jnp.float32)
+        ).astype(jnp.bfloat16)
+        p_copy(spot, side).start()
+
+    absorb(0, 1, final, False)
     top, mass = stat_rows(0)
-    result = total[0] + queries[0].astype(jnp.float32)
+    total[0] += queries[0].astype(jnp.float32)
     for spot in range(1, spots):
         s_copy(seen_from(spot)).wait_recv()
         top = jnp.maximum(top, stat_in[spot, 0:1, :])
         mass = mass + stat_in[spot, 1:2, :]
     best_ref[...] = top.astype(jnp.bfloat16)
     below = jnp.transpose(jnp.broadcast_to(1.0 + mass, (rows, rows)))[:, 0:1]
-    for spot in range(1, spots):
-        p_copy(seen_from(spot)).wait_recv()
+    for spot, _ in passing:
+        for side in range(2):
+            p_copy(seen_from(spot), side).wait_recv()
+    result = total[0]
+    for spot, _ in passing:
         result = result + part_in[spot].astype(jnp.float32)
     mean_ref[...] = (result / below).astype(jnp.bfloat16)
 
@@ -394,8 +427,11 @@
     for spot in range(1, spots):
         q_meta(spot).wait_send()
         q_copy(spot).wait_send()
-        p_copy(spot).wait_send()
         s_copy(spot).wait_send()
+    for side in range(2):
+        corner_copy(side).wait_send()
+        for spot, _ in passing:
+            p_copy(spot, side).wait_send()
 
 
 def dense(embeddings, bucket_ids, valid_rows):
@@ -428,10 +464,10 @@
             dma((planes, 2, PIECES)), dma((planes, PIECES)), dma((planes, 2)), dma((planes,)),
             dma((planes, PIECES)), dma((planes, PIECES)), dma((planes,)), dma((planes,)),
             dma((spots,)), dma((spots,)), dma((spots,)), dma((spots,)),
-            dma((spots,)), dma((spots,)), dma((spots,)), dma((spots,)),
+            dma((spots, 2)), dma((spots, 2)), dma((spots,)), dma((spots,)),
         ],
         compiler_params=pltpu.CompilerParams(
-            collective_id=0, has_side_effects=True, vmem_limit_bytes=56 * 1024 * 1024
+            collective_id=0, has_side_effects=True, vmem_limit_bytes=16 * 1024 * 1024
         ),
     )(embeddings, bucket_ids.reshape(1, rows), valid_rows.reshape(1, rows))
     return mean, best.reshape(rows)

time: 41.6 us -> 34 us (0.82)
  Pallas kernels: 38.7 us -> 30.4 us
  local copies, waits for them, and re-layouts: 2.13 us -> 2.77 us
    pallas_call x1, Pallas kernels: 38.7 us -> 30.4 us  [dense(): pl.pallas_call(functools.partial(dense_kernel, planes), out_shape=(jax.Sh...]
    unnamed x4 -> x8, local copies, waits for them, and re-layouts: 2.13 us -> 2.77 us
where the time goes in v2:
time: 34 us; the launch traced here: 33.8 us
  Pallas kernels  30.4 us (89%)
  local copies, waits for them, and re-layouts  2.77 us (8%)
  between operations  0.66 us (2%)
    pallas_call x1, Pallas kernels, dense(): pl.pallas_call(functools.partial(dense_kernel, planes), out_shape=(jax.Sh...  30.4 us
    unnamed x8, local copies, waits for them, and re-layouts  2.77 us

profile of v2, /device:TPU:0, one launch (start us, length us, event | category | flops | bytes accessed | tf_op | source)
XLA Modules:
  0.0 33.8 jit_solution(4527546395387885912)
XLA Ops:
  0.6 0.0 copy-start.1
  0.6 0.0 copy-start.2
  0.6 0.6 %copy-done.1 = s32[128]{0:T(128)S(1)} copy-done((s32[128]{0:T(128)S(1)}, s32[128]{0:T(128)}, u32[]{:S(2)}) %copy-start.1) | copy-done | bytes 536
  1.3 0.0 copy-done.2
  1.3 0.0 copy-start
  1.3 0.9 %copy-done = bf16[128,768]{1,0:T(8,128)(2,1)S(1)} copy-done((bf16[128,768]{1,0:T(8,128)(2,1)S(1)}, bf16[128,768]{1,0:T(8,128)(2,1)}, u32[]{:S(2)}) %copy-start) | copy-done | bytes 196632
  2.2 30.4 %shard_map.50 = (bf16[128,768]{1,0:T(8,128)(2,1)S(1)}, bf16[1,128]{1,0:T(2,128)(2,1)S(1)}) custom-call(bf16[128,768]{1,0:T(8,128)(2,1)S(1)} %copy-done, s32[1,128]{1,0:T(1,128)S(1)} %bitcast.3, s32[1,128]{1,0:T(1,128)S(1)} %bitcast.4), custom_call_target="tpu_custom_call" | custom-call | tf_op jit(solution)/shard_map/pallas_call | solution.py:443
  32.6 0.7 %copy.7 = bf16[128,768]{1,0:T(8,128)(2,1)} copy(bf16[128,768]{1,0:T(8,128)(2,1)S(1)} %get-tuple-element.8) | data formatting | bytes 393216
  33.3 0.5 %copy.8 = bf16[128]{0:T(256)(128)(2,1)} copy(bf16[128]{0:T(256)(128)(2,1)S(1)} %bitcast.5) | data formatting | bytes 512
Async XLA Ops:
  0.6 0.7 %copy-start.1 = (s32[128]{0:T(128)S(1)}, s32[128]{0:T(128)}, u32[]{:S(2)}) copy-start(s32[128]{0:T(128)} %param.5) | copy-start | bytes 1540
  0.6 0.7 %copy-start.2 = (s32[128]{0:T(128)S(1)}, s32[128]{0:T(128)}, u32[]{:S(2)}) copy-start(s32[128]{0:T(128)} %param.6) | copy-start | bytes 1540
  1.3 0.9 %copy-start = (bf16[128,768]{1,0:T(8,128)(2,1)S(1)}, bf16[128,768]{1,0:T(8,128)(2,1)}, u32[]{:S(2)}) copy-start(bf16[128,768]{1,0:T(8,128)(2,1)} %emb_ref.1) | copy-start | bytes 589828

commit v3 on v2

--- a/solution.py
+++ b/solution.py
@@ -127,7 +127,8 @@
 
 
 def dense_kernel(
-    planes, emb_ref, bucket_ref, valid_ref, mean_ref, best_ref,
+    planes, emb_hbm, bucket_hbm, valid_hbm, mean_ref, best_ref,
+    emb_ref, bucket_ref, valid_ref, load_sem,
     keys, key_meta, queries, query_meta, query_col, total, peak, weight,
     part_out, part_in, stat_out, stat_in,
     z_send, z_recv, zm_send, zm_recv, c_send, c_recv, cm_send, cm_recv,
@@ -162,6 +163,15 @@
     partner = at(z, y, x, other)
     has_low, has_high = z > 0, z < planes - 1
 
+    loads = [
+        pltpu.make_async_copy(source, target, load_sem.at[index])
+        for index, (source, target) in enumerate(
+            ((emb_hbm, emb_ref), (bucket_hbm, bucket_ref), (valid_hbm, valid_ref))
+        )
+    ]
+    for load in loads:
+        load.start()
+
     barrier = pltpu.get_barrier_semaphore()
 
     def greet(device):
@@ -179,6 +189,8 @@
     def _():
         greet(at(z + 1, y, x, core))
 
+    for load in loads:
+        load.wait()
     floats = emb_ref[...].astype(jnp.float32)
     inverse = lax.rsqrt(jnp.mean(floats * floats, axis=1, keepdims=True) + 1e-06)
     unit = (floats * inverse).astype(jnp.bfloat16)
@@ -446,9 +458,13 @@
             jax.ShapeDtypeStruct((rows, features), jnp.bfloat16),
             jax.ShapeDtypeStruct((1, rows), jnp.bfloat16),
         ),
-        in_specs=[vmem] * 3,
+        in_specs=[pl.BlockSpec(memory_space=pltpu.HBM)] * 3,
         out_specs=(vmem, vmem),
         scratch_shapes=[
+            pltpu.VMEM((rows, features), jnp.bfloat16),
+            pltpu.VMEM((1, rows), jnp.int32),
+            pltpu.VMEM((1, rows), jnp.int32),
+            dma((3,)),
             pltpu.VMEM((planes, PAIR, rows, features), jnp.bfloat16),
             pltpu.VMEM((planes, PAIR, 2, rows), jnp.float32),
             pltpu.VMEM((spots, rows, features), jnp.bfloat16),

time: 34 us -> 34.3 us (level)
  no operation moved by 1% of the time
where the time goes in v3:
time: 34.3 us; the launch traced here: 34.1 us
  Pallas kernels  30.7 us (90%)
  local copies, waits for them, and re-layouts  2.77 us (8%)
  between operations  0.66 us (2%)
    pallas_call x1, Pallas kernels, dense(): pl.pallas_call(functools.partial(dense_kernel, planes), out_shape=(jax.Sh...  30.7 us
    unnamed x8, local copies, waits for them, and re-layouts  2.77 us

profile of v3, /device:TPU:0, one launch (start us, length us, event | category | flops | bytes accessed | tf_op | source)
XLA Modules:
  0.0 34.1 jit_solution(2707504640720838102)
XLA Ops:
  0.6 0.0 copy-start.1
  0.6 0.0 copy-start.2
  0.6 0.6 %copy-done.1 = s32[128]{0:T(128)S(1)} copy-done((s32[128]{0:T(128)S(1)}, s32[128]{0:T(128)}, u32[]{:S(2)}) %copy-start.1) | copy-done | bytes 536
  1.3 0.0 copy-done.2
  1.3 0.0 copy-start
  1.3 0.9 %copy-done = bf16[128,768]{1,0:T(8,128)(2,1)S(1)} copy-done((bf16[128,768]{1,0:T(8,128)(2,1)S(1)}, bf16[128,768]{1,0:T(8,128)(2,1)}, u32[]{:S(2)}) %copy-start) | copy-done | bytes 196632
  2.2 30.7 %shard_map.50 = (bf16[128,768]{1,0:T(8,128)(2,1)S(1)}, bf16[1,128]{1,0:T(2,128)(2,1)S(1)}) custom-call(bf16[128,768]{1,0:T(8,128)(2,1)S(1)} %copy-done, s32[1,128]{1,0:T(1,128)S(1)} %bitcast.3, s32[1,128]{1,0:T(1,128)S(1)} %bitcast.4), custom_call_target="tpu_custom_call" | custom-call | tf_op jit(solution)/shard_map/pallas_call | solution.py:455
  32.9 0.7 %copy.7 = bf16[128,768]{1,0:T(8,128)(2,1)} copy(bf16[128,768]{1,0:T(8,128)(2,1)S(1)} %get-tuple-element.8) | data formatting | bytes 393216
  33.6 0.5 %copy.8 = bf16[128]{0:T(256)(128)(2,1)} copy(bf16[128]{0:T(256)(128)(2,1)S(1)} %bitcast.5) | data formatting | bytes 512
Async XLA Ops:
  0.6 0.7 %copy-start.1 = (s32[128]{0:T(128)S(1)}, s32[128]{0:T(128)}, u32[]{:S(2)}) copy-start(s32[128]{0:T(128)} %param.5) | copy-start | bytes 1540
  0.6 0.7 %copy-start.2 = (s32[128]{0:T(128)S(1)}, s32[128]{0:T(128)}, u32[]{:S(2)}) copy-start(s32[128]{0:T(128)} %param.6) | copy-start | bytes 1540
  1.3 0.9 %copy-start = (bf16[128,768]{1,0:T(8,128)(2,1)S(1)}, bf16[128,768]{1,0:T(8,128)(2,1)}, u32[]{:S(2)}) copy-start(bf16[128,768]{1,0:T(8,128)(2,1)} %emb_hbm.1) | copy-start | bytes 589828

commit v4 on v3

--- a/solution.py
+++ b/solution.py
@@ -113,6 +113,7 @@
 
 PAIR = 2
 PIECES = 4
+GRANT = 56_240_000
 
 
 def arrival_order(place, count):
@@ -258,10 +259,13 @@
         row = query_meta[spot, 0:1, :]
         query_col[spot] = jnp.transpose(jnp.broadcast_to(row, (rows, rows)))
 
-    def absorb(first, last, source, fresh):
+    def absorb(first, last, source, fresh, sides=tuple(range(PAIR))):
         count = (last - first) * rows
         chosen = queries[first:last].reshape(count, features)
-        block = keys[source].reshape(PAIR * rows, features)
+        if len(sides) == PAIR:
+            block = keys[source].reshape(PAIR * rows, features)
+        else:
+            block = keys[source, sides[0]]
         cosine = lax.dot_general(
             chosen, block, (((1,), (1,)), ((), ())), preferred_element_type=jnp.float32
         ) * (1.0 / features)
@@ -271,7 +275,7 @@
         factors = []
         peaks = None
         sums = None
-        for side in range(PAIR):
+        for index, side in enumerate(sides):
             key_bucket = key_meta[source, side, 0:1, :]
             key_flag = key_meta[source, side, 1:2, :]
             wanted = jnp.where(key_flag > 0, key_bucket, -1.0)
@@ -280,7 +284,7 @@
                 own = (source == z) & (core == side)
                 shift = jnp.where(own, 0, count + rows)
                 usable = usable & (line + shift != lane)
-            values = cosine[:, side * rows : (side + 1) * rows]
+            values = cosine[:, index * rows : (index + 1) * rows]
             best = jnp.where(usable, values, -1.0)
             factor = jnp.where(usable, jnp.exp(sharpness * (values - 1.0)), 0.0)
             factors.append(factor.astype(jnp.bfloat16))
@@ -355,6 +359,7 @@
     for source in sources[:-1]:
         absorb(1, spots, source, False)
     at_end(final)
+    absorb(1, spots, final, False, (core,))
     wait_partner(final)
 
     def stat_rows(spot):
@@ -388,18 +393,21 @@
             spot_device(spot),
         )
 
-    absorb(corner, corner + 1, final, False)
+    absorb(corner, corner + 1, final, False, (other,))
     part_out[corner] = total[corner].astype(jnp.bfloat16)
     corner_copy(0).start()
     corner_copy(1).start()
     passing = ((along, 1), (across, 0))
     for spot, side in passing:
-        absorb(spot, spot + 1, final, False)
+        absorb(spot, spot + 1, final, False, (other,))
         part_out[spot, halves[1 - side]] = total[spot, halves[1 - side]].astype(jnp.bfloat16)
         p_copy(spot, 1 - side).start()
     for spot in range(spots - 1, 0, -1):
         stat_out[spot] = jnp.concatenate(stat_rows(spot), axis=0)
         s_copy(spot).start()
+    absorb(0, 1, final, False)
+    top, mass = stat_rows(0)
+    total[0] += queries[0].astype(jnp.float32)
     for spot, side in passing:
         corner_copy(side).wait_recv()
         part_out[spot, halves[side]] = (
@@ -407,9 +415,6 @@
         ).astype(jnp.bfloat16)
         p_copy(spot, side).start()
 
-    absorb(0, 1, final, False)
-    top, mass = stat_rows(0)
-    total[0] += queries[0].astype(jnp.float32)
     for spot in range(1, spots):
         s_copy(seen_from(spot)).wait_recv()
         top = jnp.maximum(top, stat_in[spot, 0:1, :])
@@ -483,7 +488,7 @@
             dma((spots, 2)), dma((spots, 2)), dma((spots,)), dma((spots,)),
         ],
         compiler_params=pltpu.CompilerParams(
-            collective_id=0, has_side_effects=True, vmem_limit_bytes=16 * 1024 * 1024
+            collective_id=0, has_side_effects=True, vmem_limit_bytes=GRANT
         ),
     )(embeddings, bucket_ids.reshape(1, rows), valid_rows.reshape(1, rows))
     return mean, best.reshape(rows)

time: 34.3 us -> 33 us (0.962)
  local copies, waits for them, and re-layouts: 2.77 us -> 1.85 us
  Pallas kernels: 30.7 us -> 30.3 us
    unnamed x8 -> x6, local copies, waits for them, and re-layouts: 2.77 us -> 1.85 us
    pallas_call x1, Pallas kernels: 30.7 us -> 30.3 us  [dense(): pl.pallas_call(functools.partial(dense_kernel, planes), out_shape=(jax.Sh...]
where the time goes in v4:
time: 33 us; the launch traced here: 32.8 us
  Pallas kernels  30.3 us (92%)
  local copies, waits for them, and re-layouts  1.85 us (6%)
  between operations  0.66 us (2%)
    pallas_call x1, Pallas kernels, dense(): pl.pallas_call(functools.partial(dense_kernel, planes), out_shape=(jax.Sh...  30.3 us
    unnamed x6, local copies, waits for them, and re-layouts  1.85 us

profile of v4, /device:TPU:0, one launch (start us, length us, event | category | flops | bytes accessed | tf_op | source)
XLA Modules:
  0.0 32.8 jit_solution(2003286834119981898)
XLA Ops:
  0.6 0.0 copy-start
  0.6 0.0 copy-start.1
  0.6 0.6 %copy-done = s32[128]{0:T(128)S(1)} copy-done((s32[128]{0:T(128)S(1)}, s32[128]{0:T(128)}, u32[]{:S(2)}) %copy-start) | copy-done | bytes 536
  1.3 0.0 copy-done.1
  1.3 30.3 %shard_map.50 = (bf16[128,768]{1,0:T(8,128)(2,1)S(1)}, bf16[1,128]{1,0:T(2,128)(2,1)S(1)}) custom-call(bf16[128,768]{1,0:T(8,128)(2,1)} %emb_hbm.1, s32[1,128]{1,0:T(1,128)S(1)} %bitcast.3, s32[1,128]{1,0:T(1,128)S(1)} %bitcast.4), custom_call_target="tpu_custom_call" | custom-call | tf_op jit(solution)/shard_map/pallas_call | solution.py:460
  31.6 0.7 %copy.7 = bf16[128,768]{1,0:T(8,128)(2,1)} copy(bf16[128,768]{1,0:T(8,128)(2,1)S(1)} %get-tuple-element.8) | data formatting | bytes 393216
  32.3 0.5 %copy.8 = bf16[128]{0:T(256)(128)(2,1)} copy(bf16[128]{0:T(256)(128)(2,1)S(1)} %bitcast.5) | data formatting | bytes 512
Async XLA Ops:
  0.6 0.7 %copy-start = (s32[128]{0:T(128)S(1)}, s32[128]{0:T(128)}, u32[]{:S(2)}) copy-start(s32[128]{0:T(128)} %param.5) | copy-start | bytes 1540
  0.6 0.7 %copy-start.1 = (s32[128]{0:T(128)S(1)}, s32[128]{0:T(128)}, u32[]{:S(2)}) copy-start(s32[128]{0:T(128)} %param.6) | copy-start | bytes 1540

commit v5 on v4

--- a/solution.py
+++ b/solution.py
@@ -124,6 +124,8 @@
             order.append(place - distance)
         if distance <= high:
             order.append(place + distance)
+    if low == 0 or high == 0:
+        order = [order[1], order[1]] + order[2:]
     return order
 
 
@@ -132,8 +134,11 @@
     emb_ref, bucket_ref, valid_ref, load_sem,
     keys, key_meta, queries, query_meta, query_col, total, peak, weight,
     part_out, part_in, stat_out, stat_in,
+    plane_keys, plane_meta, help_total, help_peak, help_weight,
+    help_out, help_in, help_stat_out, help_stat_in,
     z_send, z_recv, zm_send, zm_recv, c_send, c_recv, cm_send, cm_recv,
     q_send, q_recv, qm_send, qm_recv, p_send, p_recv, s_send, s_recv,
+    f_send, f_recv, fm_send, fm_recv, h_send, h_recv,
 ):
     rows, features = emb_ref.shape
     spots = queries.shape[0]
@@ -237,11 +242,11 @@
         )
 
     def send_ways(source, act):
-        @pl.when((source <= z) & has_high)
+        @pl.when(has_high & ((source < z) | ((source == z) & (z < planes - 2))))
         def _():
             act(1, z + 1)
 
-        @pl.when((source >= z) & has_low)
+        @pl.when(has_low & ((source > z) | ((source == z) & (z > 1))))
         def _():
             act(0, z - 1)
 
@@ -259,29 +264,20 @@
         row = query_meta[spot, 0:1, :]
         query_col[spot] = jnp.transpose(jnp.broadcast_to(row, (rows, rows)))
 
-    def absorb(first, last, source, fresh, sides=tuple(range(PAIR))):
-        count = (last - first) * rows
-        chosen = queries[first:last].reshape(count, features)
-        if len(sides) == PAIR:
-            block = keys[source].reshape(PAIR * rows, features)
-        else:
-            block = keys[source, sides[0]]
+    def terms(chosen, buckets, block, metas, own_keys):
+        count = chosen.shape[0]
         cosine = lax.dot_general(
             chosen, block, (((1,), (1,)), ((), ())), preferred_element_type=jnp.float32
         ) * (1.0 / features)
-        buckets = query_col[first:last].reshape(count, rows)
         line = lax.broadcasted_iota(jnp.int32, (count, rows), 0)
         lane = lax.broadcasted_iota(jnp.int32, (count, rows), 1)
         factors = []
         peaks = None
         sums = None
-        for index, side in enumerate(sides):
-            key_bucket = key_meta[source, side, 0:1, :]
-            key_flag = key_meta[source, side, 1:2, :]
-            wanted = jnp.where(key_flag > 0, key_bucket, -1.0)
+        for index, (meta, own) in enumerate(zip(metas, own_keys)):
+            wanted = jnp.where(meta[1:2, :] > 0, meta[0:1, :], -1.0)
             usable = buckets == wanted
-            if first == 0:
-                own = (source == z) & (core == side)
+            if own is not None:
                 shift = jnp.where(own, 0, count + rows)
                 usable = usable & (line + shift != lane)
             values = cosine[:, index * rows : (index + 1) * rows]
@@ -293,6 +289,21 @@
         summed = jnp.dot(
             jnp.concatenate(factors, axis=1), block, preferred_element_type=jnp.float32
         )
+        return peaks, sums, summed
+
+    def absorb(first, last, source, fresh, sides=tuple(range(PAIR))):
+        count = (last - first) * rows
+        if len(sides) == PAIR:
+            block = keys[source].reshape(PAIR * rows, features)
+        else:
+            block = keys[source, sides[0]]
+        peaks, sums, summed = terms(
+            queries[first:last].reshape(count, features),
+            query_col[first:last].reshape(count, rows),
+            block,
+            [key_meta[source, side] for side in sides],
+            [(source == z) & (core == side) if first == 0 else None for side in sides],
+        )
         part = (last - first, rows)
         if fresh:
             peak[first:last] = peaks.reshape(*part, rows)
@@ -346,18 +357,90 @@
         for source in sources[2:]:
             take(source)
 
-    for source in sources[:-1]:
+    def each_source(act):
+        for turn, source in enumerate(sources[:-1]):
+            if turn == 1:
+
+                @pl.when(inner)
+                def _():
+                    act(source)
+            else:
+                act(source)
+
+    at_end(sources[0])
+    for source in sources[2:-1]:
         at_end(source)
+
+    def own_rows(source):
         wait_partner(source)
         absorb(0, 1, source, False)
+
+    each_source(own_rows)
+
+    def f_copies(spot):
+        return (
+            remote(
+                query_meta.at[spot], plane_meta.at[spot], fm_send.at[spot], fm_recv.at[spot], partner
+            ),
+            remote(queries.at[spot], plane_keys.at[spot], f_send.at[spot], f_recv.at[spot], partner),
+        )
+
+    helper = (z == 1) | (z == planes - 2)
+    end_z = jnp.where(z == 1, 0, planes - 1)
 
     for spot in range(1, spots):
         q_meta(seen_from(spot)).wait_recv()
         column_of(spot)
         q_copy(seen_from(spot)).wait_recv()
+
+        @pl.when(helper)
+        def _():
+            for copy in f_copies(spot):
+                copy.start()
+
+    def h_copies():
+        device = at(jnp.where(helper, end_z, z), y, x, core)
+        return (
+            remote(help_stat_out, help_stat_in, h_send.at[0], h_recv.at[0], device),
+            remote(help_out, help_in, h_send.at[1], h_recv.at[1], device),
+        )
+
     absorb(1, spots, z, True)
-    for source in sources[:-1]:
-        absorb(1, spots, source, False)
+
+    @pl.when(helper)
+    def _():
+        row = key_meta[end_z, core, 0:1, :]
+        column = jnp.transpose(jnp.broadcast_to(row, (rows, rows)))
+        for spot in range(spots):
+            if spot == 0:
+                second, second_meta = keys[z, other], key_meta[z, other]
+            else:
+                for copy in f_copies(spot):
+                    copy.wait_recv()
+                second, second_meta = plane_keys[spot], plane_meta[spot]
+            peaks, sums, summed = terms(
+                keys[end_z, core],
+                column,
+                jnp.concatenate([queries[spot], second], axis=0),
+                [query_meta[spot], second_meta],
+                [None, None],
+            )
+            if spot == 0:
+                help_peak[...] = peaks
+                help_weight[...] = sums
+                help_total[...] = summed
+            else:
+                help_peak[...] = jnp.maximum(help_peak[...], peaks)
+                help_weight[...] += sums
+                help_total[...] += summed
+        help_out[...] = help_total[...].astype(jnp.bfloat16)
+        top = jnp.max(jnp.transpose(help_peak[...]), axis=0, keepdims=True)
+        mass = jnp.sum(jnp.transpose(help_weight[...]), axis=0, keepdims=True)
+        help_stat_out[...] = jnp.concatenate([top, mass], axis=0)
+        for copy in h_copies():
+            copy.start()
+
+    each_source(lambda source: absorb(1, spots, source, False))
     at_end(final)
     absorb(1, spots, final, False, (core,))
     wait_partner(final)
@@ -406,7 +489,7 @@
         stat_out[spot] = jnp.concatenate(stat_rows(spot), axis=0)
         s_copy(spot).start()
     absorb(0, 1, final, False)
-    top, mass = stat_rows(0)
+    stat_in[0] = jnp.concatenate(stat_rows(0), axis=0)
     total[0] += queries[0].astype(jnp.float32)
     for spot, side in passing:
         corner_copy(side).wait_recv()
@@ -415,6 +498,20 @@
         ).astype(jnp.bfloat16)
         p_copy(spot, side).start()
 
+    @pl.when(jnp.logical_not(inner))
+    def _():
+        for copy in h_copies():
+            copy.wait_recv()
+        stat_in[0] = jnp.concatenate(
+            [
+                jnp.maximum(stat_in[0, 0:1, :], help_stat_in[0:1, :]),
+                stat_in[0, 1:2, :] + help_stat_in[1:2, :],
+            ],
+            axis=0,
+        )
+        total[0] += help_in[...].astype(jnp.float32)
+
+    top, mass = stat_in[0, 0:1, :], stat_in[0, 1:2, :]
     for spot in range(1, spots):
         s_copy(seen_from(spot)).wait_recv()
         top = jnp.maximum(top, stat_in[spot, 0:1, :])
@@ -435,12 +532,24 @@
     c_meta(z, core).wait_send()
     for part in range(PIECES):
         c_copy(z, core, part).wait_send()
-    for source in sources:
+    def sent(source):
         send_ways(source, lambda way, to: z_meta(source, way, to).wait_send())
         c_meta(source, core).wait_send()
         for part in range(PIECES):
             send_ways(source, lambda way, to: z_copy(source, way, to, part).wait_send())
             c_copy(source, core, part).wait_send()
+
+    each_source(sent)
+    sent(final)
+
+    @pl.when(helper)
+    def _():
+        for spot in range(1, spots):
+            for copy in f_copies(spot):
+                copy.wait_send()
+        for copy in h_copies():
+            copy.wait_send()
+
     for spot in range(1, spots):
         q_meta(spot).wait_send()
         q_copy(spot).wait_send()
@@ -482,10 +591,20 @@
             pltpu.VMEM((spots, rows, features), jnp.bfloat16),
             pltpu.VMEM((spots, 2, rows), jnp.float32),
             pltpu.VMEM((spots, 2, rows), jnp.float32),
+            pltpu.VMEM((spots, rows, features), jnp.bfloat16),
+            pltpu.VMEM((spots, 2, rows), jnp.float32),
+            pltpu.VMEM((rows, features), jnp.float32),
+            pltpu.VMEM((rows, rows), jnp.float32),
+            pltpu.VMEM((rows, rows), jnp.float32),
+            pltpu.VMEM((rows, features), jnp.bfloat16),
+            pltpu.VMEM((rows, features), jnp.bfloat16),
+            pltpu.VMEM((2, rows), jnp.float32),
+            pltpu.VMEM((2, rows), jnp.float32),
             dma((planes, 2, PIECES)), dma((planes, PIECES)), dma((planes, 2)), dma((planes,)),
             dma((planes, PIECES)), dma((planes, PIECES)), dma((planes,)), dma((planes,)),
             dma((spots,)), dma((spots,)), dma((spots,)), dma((spots,)),
             dma((spots, 2)), dma((spots, 2)), dma((spots,)), dma((spots,)),
+            dma((spots,)), dma((spots,)), dma((spots,)), dma((spots,)), dma((2,)), dma((2,)),
         ],
         compiler_params=pltpu.CompilerParams(
             collective_id=0, has_side_effects=True, vmem_limit_bytes=GRANT
@@ -500,7 +619,7 @@
     blocks = lax.axis_size("blk")
     bucket_work = blocks * (2 * rows) ** 2
     dense_work = groups * blocks * rows**2
-    fits = groups % PAIR == 0 and groups > PAIR and blocks == PAIR * PAIR and rows == 128
+    fits = groups % PAIR == 0 and groups >= 4 * PAIR and blocks == PAIR * PAIR and rows == 128
     if fits and dense_work <= 4 * bucket_work:
         return dense(embeddings, bucket_ids, valid_rows)
     return by_bucket(embeddings, bucket_ids, slot_ids, valid_rows)

time: 33 us -> 33 us (level)
  no operation moved by 1% of the time
where the time goes in v5:
time: 33 us; the launch traced here: 32.9 us
  Pallas kernels  30.4 us (92%)
  local copies, waits for them, and re-layouts  1.85 us (6%)
  between operations  0.66 us (2%)
    pallas_call x1, Pallas kernels, dense(): pl.pallas_call(functools.partial(dense_kernel, planes), out_shape=(jax.Sh...  30.4 us
    unnamed x6, local copies, waits for them, and re-layouts  1.85 us

profile of v5, /device:TPU:0, one launch (start us, length us, event | category | flops | bytes accessed | tf_op | source)
XLA Modules:
  0.0 32.9 jit_solution(534424673974680383)
XLA Ops:
  0.6 0.0 copy-start
  0.6 0.0 copy-start.1
  0.6 0.6 %copy-done = s32[128]{0:T(128)S(1)} copy-done((s32[128]{0:T(128)S(1)}, s32[128]{0:T(128)}, u32[]{:S(2)}) %copy-start) | copy-done | bytes 536
  1.3 0.0 copy-done.1
  1.3 30.4 %shard_map.50 = (bf16[128,768]{1,0:T(8,128)(2,1)S(1)}, bf16[1,128]{1,0:T(2,128)(2,1)S(1)}) custom-call(bf16[128,768]{1,0:T(8,128)(2,1)} %emb_hbm.1, s32[1,128]{1,0:T(1,128)S(1)} %bitcast.3, s32[1,128]{1,0:T(1,128)S(1)} %bitcast.4), custom_call_target="tpu_custom_call" | custom-call | tf_op jit(solution)/shard_map/pallas_call | solution.py:569
  31.7 0.7 %copy.7 = bf16[128,768]{1,0:T(8,128)(2,1)} copy(bf16[128,768]{1,0:T(8,128)(2,1)S(1)} %get-tuple-element.8) | data formatting | bytes 393216
  32.4 0.5 %copy.8 = bf16[128]{0:T(256)(128)(2,1)} copy(bf16[128]{0:T(256)(128)(2,1)S(1)} %bitcast.5) | data formatting | bytes 512
Async XLA Ops:
  0.6 0.7 %copy-start = (s32[128]{0:T(128)S(1)}, s32[128]{0:T(128)}, u32[]{:S(2)}) copy-start(s32[128]{0:T(128)} %param.5) | copy-start | bytes 1540
  0.6 0.7 %copy-start.1 = (s32[128]{0:T(128)S(1)}, s32[128]{0:T(128)}, u32[]{:S(2)}) copy-start(s32[128]{0:T(128)} %param.6) | copy-start | bytes 1540

commit v6 on v5

--- a/solution.py
+++ b/solution.py
@@ -407,6 +407,54 @@
 
     absorb(1, spots, z, True)
 
+    each_source(lambda source: absorb(1, spots, source, False))
+    at_end(final)
+    absorb(1, spots, final, False, (core,))
+    wait_partner(final)
+
+    def stat_rows(spot):
+        top = jnp.max(jnp.transpose(peak[spot]), axis=0, keepdims=True)
+        mass = jnp.sum(jnp.transpose(weight[spot]), axis=0, keepdims=True)
+        return top, mass
+
+    across, along = columns, 1
+    corner = across + along
+    half = rows // 2
+    halves = (pl.ds(0, half), pl.ds(half, half))
+
+    def p_copy(spot, side):
+        mine = seen_from(spot)
+        return remote(
+            part_out.at[spot, halves[side]], part_in.at[mine, halves[side]],
+            p_send.at[spot, side], p_recv.at[mine, side], spot_device(spot),
+        )
+
+    def corner_copy(side):
+        spot = (along, across)[side]
+        return remote(
+            part_out.at[corner, halves[side]], part_in.at[corner, halves[side]],
+            p_send.at[corner, side], p_recv.at[corner, side], spot_device(spot),
+        )
+
+    def s_copy(spot):
+        mine = seen_from(spot)
+        return remote(
+            stat_out.at[spot], stat_in.at[mine], s_send.at[spot], s_recv.at[mine],
+            spot_device(spot),
+        )
+
+    absorb(corner, corner + 1, final, False, (other,))
+    part_out[corner] = total[corner].astype(jnp.bfloat16)
+    corner_copy(0).start()
+    corner_copy(1).start()
+    passing = ((along, 1), (across, 0))
+    for spot, side in passing:
+        absorb(spot, spot + 1, final, False, (other,))
+        part_out[spot, halves[1 - side]] = total[spot, halves[1 - side]].astype(jnp.bfloat16)
+        p_copy(spot, 1 - side).start()
+    for spot in range(spots - 1, 0, -1):
+        stat_out[spot] = jnp.concatenate(stat_rows(spot), axis=0)
+        s_copy(spot).start()
     @pl.when(helper)
     def _():
         row = key_meta[end_z, core, 0:1, :]
@@ -440,63 +488,16 @@
         for copy in h_copies():
             copy.start()
 
-    each_source(lambda source: absorb(1, spots, source, False))
-    at_end(final)
-    absorb(1, spots, final, False, (core,))
-    wait_partner(final)
-
-    def stat_rows(spot):
-        top = jnp.max(jnp.transpose(peak[spot]), axis=0, keepdims=True)
-        mass = jnp.sum(jnp.transpose(weight[spot]), axis=0, keepdims=True)
-        return top, mass
-
-    across, along = columns, 1
-    corner = across + along
-    half = rows // 2
-    halves = (pl.ds(0, half), pl.ds(half, half))
-
-    def p_copy(spot, side):
-        mine = seen_from(spot)
-        return remote(
-            part_out.at[spot, halves[side]], part_in.at[mine, halves[side]],
-            p_send.at[spot, side], p_recv.at[mine, side], spot_device(spot),
-        )
-
-    def corner_copy(side):
-        spot = (along, across)[side]
-        return remote(
-            part_out.at[corner, halves[side]], part_in.at[corner, halves[side]],
-            p_send.at[corner, side], p_recv.at[corner, side], spot_device(spot),
-        )
-
-    def s_copy(spot):
-        mine = seen_from(spot)
-        return remote(
-            stat_out.at[spot], stat_in.at[mine], s_send.at[spot], s_recv.at[mine],
-            spot_device(spot),
-        )
-
-    absorb(corner, corner + 1, final, False, (other,))
-    part_out[corner] = total[corner].astype(jnp.bfloat16)
-    corner_copy(0).start()
-    corner_copy(1).start()
-    passing = ((along, 1), (across, 0))
-    for spot, side in passing:
-        absorb(spot, spot + 1, final, False, (other,))
-        part_out[spot, halves[1 - side]] = total[spot, halves[1 - side]].astype(jnp.bfloat16)
-        p_copy(spot, 1 - side).start()
-    for spot in range(spots - 1, 0, -1):
-        stat_out[spot] = jnp.concatenate(stat_rows(spot), axis=0)
-        s_copy(spot).start()
-    absorb(0, 1, final, False)
-    stat_in[0] = jnp.concatenate(stat_rows(0), axis=0)
-    total[0] += queries[0].astype(jnp.float32)
     for spot, side in passing:
         corner_copy(side).wait_recv()
         part_out[spot, halves[side]] = (
             total[spot, halves[side]] + part_in[corner, halves[side]].astype(jnp.float32)
         ).astype(jnp.bfloat16)
         p_copy(spot, side).start()
+
+    absorb(0, 1, final, False)
+    stat_in[0] = jnp.concatenate(stat_rows(0), axis=0)
+    total[0] += queries[0].astype(jnp.float32)
 
     @pl.when(jnp.logical_not(inner))
     def _():

time: 33 us -> 32.6 us (0.988)
  Pallas kernels: 30.4 us -> 29.9 us
    pallas_call x1, Pallas kernels: 30.4 us -> 29.9 us  [dense(): pl.pallas_call(functools.partial(dense_kernel, planes), out_shape=(jax.Sh...]
where the time goes in v6:
time: 32.6 us; the launch traced here: 32.4 us
  Pallas kernels  29.9 us (92%)
  local copies, waits for them, and re-layouts  1.85 us (6%)
  between operations  0.66 us (2%)
    pallas_call x1, Pallas kernels, dense(): pl.pallas_call(functools.partial(dense_kernel, planes), out_shape=(jax.Sh...  29.9 us
    unnamed x6, local copies, waits for them, and re-layouts  1.85 us

profile of v6, /device:TPU:0, one launch (start us, length us, event | category | flops | bytes accessed | tf_op | source)
XLA Modules:
  0.0 32.4 jit_solution(17758499344465518930)
XLA Ops:
  0.6 0.0 copy-start
  0.6 0.0 copy-start.1
  0.6 0.6 %copy-done = s32[128]{0:T(128)S(1)} copy-done((s32[128]{0:T(128)S(1)}, s32[128]{0:T(128)}, u32[]{:S(2)}) %copy-start) | copy-done | bytes 536
  1.3 0.0 copy-done.1
  1.3 29.9 %shard_map.50 = (bf16[128,768]{1,0:T(8,128)(2,1)S(1)}, bf16[1,128]{1,0:T(2,128)(2,1)S(1)}) custom-call(bf16[128,768]{1,0:T(8,128)(2,1)} %emb_hbm.1, s32[1,128]{1,0:T(1,128)S(1)} %bitcast.3, s32[1,128]{1,0:T(1,128)S(1)} %bitcast.4), custom_call_target="tpu_custom_call" | custom-call | tf_op jit(solution)/shard_map/pallas_call | solution.py:570
  31.3 0.7 %copy.7 = bf16[128,768]{1,0:T(8,128)(2,1)} copy(bf16[128,768]{1,0:T(8,128)(2,1)S(1)} %get-tuple-element.8) | data formatting | bytes 393216
  31.9 0.5 %copy.8 = bf16[128]{0:T(256)(128)(2,1)} copy(bf16[128]{0:T(256)(128)(2,1)S(1)} %bitcast.5) | data formatting | bytes 512
Async XLA Ops:
  0.6 0.7 %copy-start = (s32[128]{0:T(128)S(1)}, s32[128]{0:T(128)}, u32[]{:S(2)}) copy-start(s32[128]{0:T(128)} %param.5) | copy-start | bytes 1540
  0.6 0.7 %copy-start.1 = (s32[128]{0:T(128)S(1)}, s32[128]{0:T(128)}, u32[]{:S(2)}) copy-start(s32[128]{0:T(128)} %param.6) | copy-start | bytes 1540
